TPU v7x, 512 devices: a whole 4x8x8 slice. The times are simulated.
512 devices in a mesh: section: 4 (over x), seq: 8 (over y), dp: 16 (over z, core).
Axes of the slice: x: 4, y: 8, z: 8, core: 2. Of those that a mesh axis runs over, the one named last changes fastest.
Arguments:
- queries: bfloat16 [16, 1024, 32, 128], P('dp', 'seq', 'section'), may hold values from -18 to 18
- video_keys: bfloat16 [16, 1024, 32, 128], P('dp', 'seq', 'section'), may hold values from -18 to 18
- video_values: bfloat16 [16, 1024, 32, 128], P('dp', 'seq', 'section'), may hold values from -6 to 6
- cross_queries: bfloat16 [16, 1024, 32, 128], P('dp', 'seq', 'section'), may hold values from -8 to 8
- self_cotangent: bfloat16 [16, 1024, 32, 128], P('dp', 'seq', 'section'), may hold values from -6 to 6
- cross_cotangent: bfloat16 [16, 1024, 32, 128], P('dp', 'seq', 'section'), may hold values from -6 to 6
- caption_states: bfloat16 [16, 512, 4096], P('dp', 'seq'), may hold values from -400 to 400
- caption_gain: float32 [4096], replicated, may hold values from 0.25 to 1.75
- key_weight: bfloat16 [4096, 4096], P('dp', ('section', 'seq')), may hold values from -0.09375 to 0.09375
- value_weight: bfloat16 [4096, 4096], P('dp', ('section', 'seq')), may hold values from -0.09375 to 0.09375
- video_length: int32 [16], replicated, may hold values from 512 to 1024, as said below
- caption_length: int32 [16], replicated, may hold values from 128 to 512, as said below
Outputs:
- query_gradient: bfloat16 [16, 1024, 32, 128], P('dp', 'seq', 'section')
- key_gradient: bfloat16 [16, 1024, 32, 128], P('dp', 'seq', 'section')
- value_gradient: bfloat16 [16, 1024, 32, 128], P('dp', 'seq', 'section')
- cross_query_gradient: bfloat16 [16, 1024, 32, 128], P('dp', 'seq', 'section')
- key_weight_gradient: float32 [4096, 4096], P('dp', ('section', 'seq'))
- value_weight_gradient: float32 [4096, 4096], P('dp', ('section', 'seq'))
Inputs may be any that keep to these rules, and one draw needn't show every extreme that they name: `video_length`: some clip has all 1024 tokens valid. `caption_length`: some clip has all 512 caption tokens valid.
All inputs are finite; a program needn't handle non-finite values.
Results may differ from a plain program's by a relative error of at most 0.018.
Values may be sent and summed in bfloat16 or wider, within the bound.
A program may use at most 64 MiB of HBM per device.

v0:
```python
import math
import jax
import jax.numpy as jnp
from jax import lax
from jax.sharding import PartitionSpec as P

norm_epsilon = 1e-06


def sent_together(arrays, axis, dim, along):
    ends, at = ([], 0)
    for a in arrays[:-1]:
        at += a.shape[along]
        ends.append(at)
    both = jnp.concatenate(arrays, axis=along)
    return tuple(jnp.split(lax.all_gather(both, axis, axis=dim, tiled=True), ends, axis=along))


def side_by_side(arrays, axis, split_dim, concat_dim, along):
    widths = [a.shape[along] for a in arrays]
    both = jnp.concatenate(arrays, axis=along)
    out = lax.all_to_all(both, axis, split_axis=split_dim, concat_axis=concat_dim, tiled=True)
    return tuple(jnp.split(out, [sum(widths[:k]) for k in range(1, len(widths))], axis=along))


def normalize_rows(states, caption_gain):
    values = states.astype(jnp.float32)
    mean_square = jnp.mean(values * values, axis=-1, keepdims=True)
    return (values * lax.rsqrt(mean_square + norm_epsilon) * caption_gain).astype(jnp.bfloat16)


def block_gradients(query_rows, cotangent_rows, key_rows, value_rows, key_limit, score_scale):
    scores = (
        jnp.einsum("qhd,khd->hqk", query_rows, key_rows, preferred_element_type=jnp.float32)
        * score_scale
    )
    columns = lax.broadcasted_iota(jnp.int32, scores.shape, 2)
    scores = jnp.where(columns < key_limit, scores, -jnp.inf)
    maxima = jnp.max(scores, axis=-1, keepdims=True)
    powers = jnp.exp(scores - maxima)
    weights = powers / jnp.sum(powers, axis=-1, keepdims=True)
    weights_low = weights.astype(jnp.bfloat16)
    weight_grad = jnp.einsum(
        "qhd,khd->hqk", cotangent_rows, value_rows, preferred_element_type=jnp.float32
    )
    row_total = jnp.sum(weights * weight_grad, axis=-1, keepdims=True)
    score_grad = (weights * (weight_grad - row_total) * score_scale).astype(jnp.bfloat16)
    query_grad = jnp.einsum(
        "hqk,khd->qhd", score_grad, key_rows, preferred_element_type=jnp.float32
    )
    key_grad = jnp.einsum(
        "hqk,qhd->khd", score_grad, query_rows, preferred_element_type=jnp.float32
    )
    value_grad = jnp.einsum(
        "hqk,qhd->khd", weights_low, cotangent_rows, preferred_element_type=jnp.float32
    )
    return (query_grad, key_grad, value_grad)


def attention_gradients(query_set, cotangent_set, key_set, value_set, key_limit, score_scale):
    row_count = query_set.shape[0]
    block_rows = math.gcd(row_count, 512)
    block_count = row_count // block_rows
    query_blocks = query_set.reshape((block_count, block_rows) + query_set.shape[1:])
    cotangent_blocks = cotangent_set.reshape((block_count, block_rows) + cotangent_set.shape[1:])

    def advance(totals, inputs):
        query_grad, key_grad, value_grad = block_gradients(
            inputs[0], inputs[1], key_set, value_set, key_limit, score_scale
        )
        return ((totals[0] + key_grad, totals[1] + value_grad), query_grad)

    empty = jnp.zeros(key_set.shape, jnp.float32)
    totals, query_grads = lax.scan(advance, (empty, empty), (query_blocks, cotangent_blocks))
    return (query_grads.reshape(query_set.shape), totals[0], totals[1])


def local(
    queries,
    video_keys,
    video_values,
    cross_queries,
    self_cotangent,
    cross_cotangent,
    caption_states,
    caption_gain,
    key_weight,
    value_weight,
    video_length,
    caption_length,
):
    head_size = queries.shape[3]
    score_scale = 1.0 / math.sqrt(head_size)
    head_width = key_weight.shape[1]
    local_heads = head_width // head_size
    normed = normalize_rows(lax.all_gather(caption_states, "seq", axis=1, tiled=True), caption_gain)
    normed_text = normed[0]
    caption_rows = normed_text.shape[0]
    pieces = sent_together((key_weight, value_weight), "dp", 0, 1)
    columns = normed_text
    text_keys = jnp.dot(columns, pieces[0], preferred_element_type=jnp.float32)
    text_values = jnp.dot(columns, pieces[1], preferred_element_type=jnp.float32)
    text_keys = text_keys.astype(jnp.bfloat16).reshape(caption_rows, local_heads, head_size)
    text_values = text_values.astype(jnp.bfloat16).reshape(caption_rows, local_heads, head_size)
    gathered = side_by_side(
        (queries, video_keys, video_values, cross_queries, self_cotangent, cross_cotangent),
        "seq",
        2,
        1,
        0,
    )
    head_queries, head_keys, head_values, head_cross, self_rows, cross_rows = (
        tensor[0] for tensor in gathered
    )
    clip_index = lax.axis_index("dp")
    video_limit = lax.dynamic_index_in_dim(video_length, clip_index, 0, keepdims=False)
    caption_limit = lax.dynamic_index_in_dim(caption_length, clip_index, 0, keepdims=False)
    positions = lax.broadcasted_iota(jnp.int32, (head_queries.shape[0], 1, 1), 0)
    nothing = jnp.zeros((), jnp.bfloat16)
    self_rows = jnp.where(positions < video_limit, self_rows, nothing)
    cross_rows = jnp.where(positions < video_limit, cross_rows, nothing)
    query_grad, key_grad, value_grad = attention_gradients(
        head_queries, self_rows, head_keys, head_values, video_limit, score_scale
    )
    cross_grad, text_key_grad, text_value_grad = attention_gradients(
        head_cross, cross_rows, text_keys, text_values, caption_limit, score_scale
    )
    returned = side_by_side(
        (
            query_grad.astype(jnp.bfloat16)[None],
            key_grad.astype(jnp.bfloat16)[None],
            value_grad.astype(jnp.bfloat16)[None],
            cross_grad.astype(jnp.bfloat16)[None],
        ),
        "seq",
        1,
        2,
        0,
    )
    key_cot = text_key_grad.astype(jnp.bfloat16).reshape(caption_rows, head_width)
    value_cot = text_value_grad.astype(jnp.bfloat16).reshape(caption_rows, head_width)
    stacked = jnp.concatenate((key_cot, value_cot), axis=1)
    contract_rows = (((0,), (0,)), ((), ()))
    columns = normed_text
    gradients = lax.psum_scatter(
        lax.dot_general(columns, stacked, contract_rows, preferred_element_type=jnp.float32).astype(
            jnp.bfloat16
        ),
        "dp",
        scatter_dimension=0,
        tiled=True,
    ).astype(jnp.float32)
    return (
        returned[0],
        returned[1],
        returned[2],
        returned[3],
        gradients[:, :head_width],
        gradients[:, head_width:],
    )


def solution(mesh):
    placed = (
        P("dp", "seq", "section", None),
        P("dp", "seq", "section", None),
        P("dp", "seq", "section", None),
        P("dp", "seq", "section", None),
        P("dp", "seq", "section", None),
        P("dp", "seq", "section", None),
        P("dp", "seq", None),
        P(),
        P("dp", ("section", "seq")),
        P("dp", ("section", "seq")),
        P(),
        P(),
    )
    return jax.shard_map(
        local,
        mesh=mesh,
        in_specs=placed,
        out_specs=(
            P("dp", "seq", "section", None),
            P("dp", "seq", "section", None),
            P("dp", "seq", "section", None),
            P("dp", "seq", "section", None),
            P("dp", ("section", "seq")),
            P("dp", ("section", "seq")),
        ),
        check_vma=False,
    )
```

profile of v0, /device:TPU:12, one launch (start us, length us, event | category | flops | bytes accessed | tf_op | source)
XLA Modules:
  0.0 239.1 jit_solution(1283080764883097908)
XLA Ops:
  8.0 1.5 pad_maximum_fusion.1
  9.6 1.7 copy_dynamic-update-slice_fusion.5
  11.3 1.7 copy_dynamic-update-slice_fusion.4
  13.8 0.8 copy_dynamic-update-slice_fusion.2
  14.5 0.8 copy_dynamic-update-slice_fusion.1
  16.1 7.5 %all-to-all-start = ((bf16[6,128,8,128]{3,1,0,2:T(8,128)(2,1)}), bf16[6,128,8,128]{3,1,0,2:T(8,128)(2,1)S(1)}, u32[]{:S(2)}, u32[]{:S(2)}) async-start(bf16[6,128,8,128]{3,1,0,2:T(8,128)(2,1)} %copy_dynamic-update-slice_fusion), calls=%async_computation | async-start | bytes 3145728 | tf_op jit(solution)/shard_map/all_to_all | solution.py:22
  25.5 50.6 %all-to-all-done = bf16[6,128,8,128]{3,1,0,2:T(8,128)(2,1)S(1)} async-done(((bf16[6,128,8,128]{3,1,0,2:T(8,128)(2,1)}), bf16[6,128,8,128]{3,1,0,2:T(8,128)(2,1)S(1)}, u32[]{:S(2)}, u32[]{:S(2)}) %all-to-all-start) | async-done | bytes 1572896 | tf_op jit(solution)/shard_map/all_to_all | solution.py:22
  76.2 0.8 fusion.65
  77.1 0.9 select_bitcast_fusion.1
  78.0 21.0 %all-gather.3.cloned.1.call-done = bf16[1,512,4096]{2,1,0:T(8,128)(2,1)} async-done(((bf16[1,64,4096]{2,1,0:T(8,128)(2,1)}), bf16[1,512,4096]{2,1,0:T(8,128)(2,1)}) %all-gather.3.cloned.1.call-update) | async-done | bytes 4194320 | tf_op jit(solution)/shard_map/all_gather | solution.py:96
  99.0 3.1 %fusion.49 = f32[512]{0:T(512)S(1)} fusion(bf16[1,512,4096]{2,1,0:T(8,128)(2,1)} %all-gather.3.cloned.1.call-done), kind=kLoop, calls=%fused_computation.65 | loop fusion | flops 6290944 | bytes 4196352 | tf_op jit(solution)/shard_map/reduce_sum | solution.py:28
  102.1 45.8 %all-gather.5.cloned.1.call-done = bf16[4096,256]{1,0:T(8,128)(2,1)} async-done(((bf16[256,256]{1,0:T(8,128)(2,1)}), bf16[4096,256]{1,0:T(8,128)(2,1)}) %all-gather.5.cloned.1.call-update) | async-done | bytes 2097168 | tf_op jit(solution)/shard_map/all_gather | solution.py:16
  147.9 3.9 %fusion.53 = bf16[512,1,128]{2,0,1:T(8,128)(2,1)S(1)} fusion(bf16[4096,256]{1,0:T(8,128)(2,1)} %all-gather.5.cloned.1.call-done, bf16[1,512,4096]{2,1,0:T(8,128)(2,1)} %all-gather.3.cloned.1.call-done, f32[4096]{0:T(1024)S(1)} %copy-done.9, f32[512]{0:T(512)S(1)} %add_rsqrt_fusion), kind=kOutput, calls=%fused_computation.73 | convolution fusion | flops 545325056 | bytes 5392384 | tf_op jit(solution)/shard_map/dot_general | solution.py:101
  152.4 1.3 fusion.54
  153.7 8.4 %while.31 = (s32[]{:T(128)}, f32[512,1,128]{0,2,1:T(8,128)}, f32[512,1,128]{0,2,1:T(8,128)S(1)}, bf16[2,512,1,128]{3,1,2,0:T(8,128)(2,1)S(1)}, bf16[2,512,1,128]...) while((s32[]{:T(128)}, f32[512,1,128]{0,2,1:T(8,128)}, ...), condition=%wide.region_10.11_spmd.clone, body=%wide.region_6.10_spmd.clone.sunk | while | flops 340524032 | bytes 11164816 | solution.py:74
  156.1 1.0 fusion.112
  159.8 2.0 fusion.112
  162.2 1.1 convert_bitcast_fusion.2
  163.3 5.2 %convolution_convert_fusion = bf16[4096,256]{1,0:T(8,128)(2,1)} fusion(bf16[512,128]{0,1:T(8,128)(2,1)S(1)} %get-tuple-element.309, bf16[512,128]{0,1:T(8,128)(2,1)S(1)} %get-tuple-element.310, bf16[1,512,4096]{2,1,0:T(8,128)(2,1)} %all-gather.3.cloned.1.call-done, f32[4096]{0:T(1024)S(1)} %copy-done.9, f32[512]{0:T(512)S(1)} %add_rsqrt_fusion), kind=kOutput, calls=%fused_computation.68 | convolution fusion | flops 1083703296 | bytes 6572032 | tf_op jit(solution)/shard_map/dot_general | solution.py:146
  168.6 13.7 %while.30 = (s32[]{:T(128)}, f32[1024,1,128]{0,2,1:T(8,128)S(1)}, f32[1024,1,128]{0,2,1:T(8,128)}, bf16[2,512,1,128]{3,1,2,0:T(8,128)(2,1)S(1)}, bf16[2,512,1,12...) while((s32[]{:T(128)}, f32[1024,1,128]{0,2,1:T(8,128)S(1)}, ...), condition=%wide.region_4.5_spmd.clone, body=%wide.region_0.4_spmd.clone.sunk | while | flops 685243904 | bytes 23622340 | solution.py:74
  170.4 2.6 %fusion.102 = f32[1024,1,128]{0,2,1:T(8,128)} fusion(f32[1024,1,128]{0,2,1:T(8,128)} %get-tuple-element.483, pred[]{:T(512)S(6)} %compare.6, bf16[2,512,1,128]{3,1,2,0:T(8,128)(2,1)} %get-tuple-element.499, s32[]{:T(128)} %get-tuple-element.481, f32[512,1024]{1,0:T(8,128)S(1)} %get-tuple-element.420, f32[512]{0:T(512)S(1)} %fusion.100, ...), kind=kOutput, calls=%fused_computation.10.clone.1 | convolution fusion | flops 137101312 | bytes 3282433 | tf_op jit(solution)/shard_map/while/body/eval_jaxpr/hqk,qhd->khd/dot_general | solution.py:54
  177.1 2.8 %fusion.102 = f32[1024,1,128]{0,2,1:T(8,128)} fusion(f32[1024,1,128]{0,2,1:T(8,128)} %get-tuple-element.483, pred[]{:T(512)S(6)} %compare.6, bf16[2,512,1,128]{3,1,2,0:T(8,128)(2,1)} %get-tuple-element.499, s32[]{:T(128)} %get-tuple-element.481, f32[512,1024]{1,0:T(8,128)S(1)} %get-tuple-element.420, f32[512]{0:T(512)S(1)} %fusion.100, ...), kind=kOutput, calls=%fused_computation.10.clone.1 | convolution fusion | flops 137101312 | bytes 3282433 | tf_op jit(solution)/shard_map/while/body/eval_jaxpr/hqk,qhd->khd/dot_general | solution.py:54
  182.3 1.2 copy.73
  183.7 1.1 pad_maximum_fusion
  184.8 0.8 copy.77
  185.6 34.7 %all_to_all.30 = bf16[4,1024,1,128]{3,0,2,1:T(4,128)(2,1)S(1)} all-to-all(bf16[4,1024,1,128]{3,0,2,1:T(4,128)(2,1)S(1)} %copy.77), channel_id=1, replica_groups=mesh['section'=4,'seq'=8,'dp'=16] {'seq'}, dimensions={1} | all-to-all | bytes 2097152 | tf_op jit(solution)/shard_map/all_to_all | solution.py:22
  220.5 0.9 copy.79
  221.4 0.9 copy.80
  222.3 0.9 copy.81
  223.2 0.9 copy.82
  224.0 6.9 %reduce-scatter.2.cloned.1.call-done = bf16[256,256]{1,0:T(8,128)(2,1)} async-done(((bf16[4096,256]{1,0:T(8,128)(2,1)}), bf16[256,256]{1,0:T(8,128)(2,1)}) %reduce-scatter.2.cloned.1.call-update) | async-done | bytes 131088 | tf_op jit(solution)/shard_map/reduce_scatter | solution.py:145
  230.9 1.6 fusion.66
  (78 shorter events, 18.7 us)
Async XLA Ops:
  7.2 5.8 %copy-start.3 = (bf16[1,128,8,128]{3,2,1,0:T(8,128)(2,1)S(1)}, bf16[1,128,8,128]{3,2,1,0:T(8,128)(2,1)}, u32[]{:S(2)}) copy-start(bf16[1,128,8,128]{3,2,1,0:T(8,128)(2,1)} %param.18) | copy-start | bytes 786436
  7.2 6.6 %copy-start.4 = (bf16[1,128,8,128]{3,2,1,0:T(8,128)(2,1)S(1)}, bf16[1,128,8,128]{3,2,1,0:T(8,128)(2,1)}, u32[]{:S(2)}) copy-start(bf16[1,128,8,128]{3,2,1,0:T(8,128)(2,1)} %param.19) | copy-start | bytes 786436
  7.2 7.3 %copy-start.5 = (bf16[1,128,8,128]{3,2,1,0:T(8,128)(2,1)S(1)}, bf16[1,128,8,128]{3,2,1,0:T(8,128)(2,1)}, u32[]{:S(2)}) copy-start(bf16[1,128,8,128]{3,2,1,0:T(8,128)(2,1)} %param.20) | copy-start | bytes 786436
  7.2 8.1 %copy-start.6 = (bf16[1,128,8,128]{3,2,1,0:T(8,128)(2,1)S(1)}, bf16[1,128,8,128]{3,2,1,0:T(8,128)(2,1)}, u32[]{:S(2)}) copy-start(bf16[1,128,8,128]{3,2,1,0:T(8,128)(2,1)} %param.21) | copy-start | bytes 786436
  7.2 91.8 %all-gather.3.cloned.1.call-start = ((), (), s32[]{:S(2)}) async-start(), calls=%async_computation.3 | async-start | bytes 4718592 | tf_op jit(solution)/shard_map/all_gather | solution.py:96
  7.9 140.0 %all-gather.5.cloned.1.call-start = ((), (), s32[]{:S(2)}) async-start(), calls=%async_computation.4 | async-start | bytes 2228224 | tf_op jit(solution)/shard_map/all_gather | solution.py:16
  14.5 9.1 %copy-start.10 = (s32[16]{0:T(128)S(1)}, s32[16]{0:T(128)}, u32[]{:S(2)}) copy-start(s32[16]{0:T(128)} %param.26) | copy-start | bytes 196
  14.5 9.8 %copy-start.11 = (s32[16]{0:T(128)S(1)}, s32[16]{0:T(128)}, u32[]{:S(2)}) copy-start(s32[16]{0:T(128)} %param.27) | copy-start | bytes 196
  16.1 60.0 %all-to-all-start = ((bf16[6,128,8,128]{3,1,0,2:T(8,128)(2,1)}), bf16[6,128,8,128]{3,1,0,2:T(8,128)(2,1)S(1)}, u32[]{:S(2)}, u32[]{:S(2)}) async-start(bf16[6,128,8,128]{3,1,0,2:T(8,128)(2,1)} %copy_dynamic-update-slice_fusion), calls=%async_computation | async-start | bytes 3145728 | tf_op jit(solution)/shard_map/all_to_all | solution.py:22
  23.6 207.3 %reduce-scatter.2.cloned.1.call-start = ((), (), s32[]{:S(2)}) async-start(), calls=%async_computation.5 | async-start | bytes 2228224 | tf_op jit(solution)/shard_map/reduce_scatter | solution.py:145
  78.0 70.0 %copy-start.9 = (f32[4096]{0:T(1024)S(1)}, f32[4096]{0:T(1024)}, u32[]{:S(2)}) copy-start(f32[4096]{0:T(1024)} %param.23) | copy-start | bytes 49156
  147.9 4.0 %copy-start = (bf16[1,512,4096]{2,1,0:T(8,128)(2,1)S(1)}, bf16[1,512,4096]{2,1,0:T(8,128)(2,1)}, u32[]{:S(2)}) copy-start(bf16[1,512,4096]{2,1,0:T(8,128)(2,1)} %all-gather.3.cloned.1.call-done) | copy-start | bytes 12582916
  147.9 4.4 %copy-start.8 = (bf16[4096,256]{1,0:T(8,128)(2,1)S(1)}, bf16[4096,256]{1,0:T(8,128)(2,1)}, u32[]{:S(2)}) copy-start(bf16[4096,256]{1,0:T(8,128)(2,1)} %all-gather.5.cloned.1.call-done) | copy-start | bytes 6291460
  162.2 6.3 %copy-start.1 = (bf16[2,512,1,128]{3,1,2,0:T(8,128)(2,1)}, bf16[2,512,1,128]{3,1,2,0:T(8,128)(2,1)S(1)}, u32[]{:S(2)}) copy-start(bf16[2,512,1,128]{3,1,2,0:T(8,128)(2,1)S(1)} %get-tuple-element.107) | copy-start | bytes 786436
  170.3 2.6 %copy-start.2 = (bf16[1024,1,128]{2,0,1:T(8,128)(2,1)S(1)}, bf16[1024,1,128]{2,0,1:T(8,128)(2,1)}, u32[]{:S(2)}) copy-start(bf16[1024,1,128]{2,0,1:T(8,128)(2,1)} %get-tuple-element.500) | copy-start | bytes 786436 | tf_op jit(solution)/shard_map/while
  170.3 2.6 %copy-start.7 = (bf16[2,512,1,128]{3,1,2,0:T(8,128)(2,1)S(1)}, bf16[2,512,1,128]{3,1,2,0:T(8,128)(2,1)}, u32[]{:S(2)}) copy-start(bf16[2,512,1,128]{3,1,2,0:T(8,128)(2,1)} %get-tuple-element.499) | copy-start | bytes 786436 | tf_op jit(solution)/shard_map/while
  177.1 2.8 %copy-start.2 = (bf16[1024,1,128]{2,0,1:T(8,128)(2,1)S(1)}, bf16[1024,1,128]{2,0,1:T(8,128)(2,1)}, u32[]{:S(2)}) copy-start(bf16[1024,1,128]{2,0,1:T(8,128)(2,1)} %get-tuple-element.500) | copy-start | bytes 786436 | tf_op jit(solution)/shard_map/while
  177.1 2.8 %copy-start.7 = (bf16[2,512,1,128]{3,1,2,0:T(8,128)(2,1)S(1)}, bf16[2,512,1,128]{3,1,2,0:T(8,128)(2,1)}, u32[]{:S(2)}) copy-start(bf16[2,512,1,128]{3,1,2,0:T(8,128)(2,1)} %get-tuple-element.499) | copy-start | bytes 786436 | tf_op jit(solution)/shard_map/while
Sparse Core Ops, SparseCore 0:
  10.1 88.8 all-gather.2
  101.7 46.1 all-gather.4
  168.7 62.2 reduce-scatter.1
where the time goes:
time: 240 us; the launch traced here: 239 us
  waiting for transfers between devices  125 us (52%)
  blocking collectives  34.7 us (14%)
  matrix products  26 us (11%)
  local copies, waits for them, and re-layouts  16.8 us (7%)
  other arithmetic  14.5 us (6%)
  between operations  13.9 us (6%)
  starting transfers between devices  7.62 us (3%)
    all_to_all x1, waiting for transfers between devices, side_by_side(): lax.all_to_all(both, axis, split_axis=split_dim, concat_axis=concat_dim,...  50.6 us
    all_gather x1, waiting for transfers between devices, sent_together(): lax.all_gather(both, axis, axis=dim, tiled=True)  45.8 us
    all_to_all x1, blocking collectives, side_by_side(): lax.all_to_all(both, axis, split_axis=split_dim, concat_axis=concat_dim,...  34.7 us
    all_gather x1, waiting for transfers between devices, local(): lax.all_gather(caption_states, 'seq', axis=1, tiled=True)  21 us
    unnamed x29, local copies, waits for them, and re-layouts  9.77 us
    all_to_all x1, starting transfers between devices, side_by_side(): lax.all_to_all(both, axis, split_axis=split_dim, concat_axis=concat_dim,...  7.55 us
    reduce_scatter x1, waiting for transfers between devices, local(): lax.psum_scatter(lax.dot_general(columns, stacked, contract_rows, preferr...  6.91 us
    dot_general x4, matrix products, block_gradients(): jnp.einsum('hqk,qhd->khd', weights_low, cotangent_rows, preferred_element...  6.08 us
  transfers between devices with their start and end apart: 4, of which 4 were waited for; matrix products, arithmetic and copies ran while one was open for 15% of the time, Pallas kernels for 0%

commit v1 on v0

--- a/solution.py
+++ b/solution.py
@@ -1,3 +1,4 @@
+import functools
 import math
 import jax
 import jax.numpy as jnp
@@ -5,6 +6,39 @@
 from jax.sharding import PartitionSpec as P
 
 norm_epsilon = 1e-06
+
+
+def clear_modes(message, d0):
+    p_next = list(message.shape[1:])
+    p_next[d0] *= message.shape[0]
+    return jnp.moveaxis(message, 0, d0).reshape(p_next)
+
+
+def read_rates(arr_in, ax_name, which_dim):
+    axis_len = jax.lax.axis_size(ax_name)
+    inbox = []
+    for b in tuple(range(axis_len)):
+        inbox.append((b, (b + 1) % axis_len))
+    by_rank = []
+    for nth, num in inbox:
+        by_rank.append((num, nth))
+    block_out, k_now = ([], [])
+    for m in tuple(range(axis_len - 1)):
+        if m % 2 == 0:
+            z = jax.lax.ppermute(block_out[-1] if block_out else arr_in, ax_name, inbox)
+            block_out.append(z)
+        else:
+            back = jax.lax.ppermute(k_now[-1] if k_now else arr_in, perm=by_rank, axis_name=ax_name)
+            k_now.append(back)
+    piece_next = jnp.stack([*block_out[::-1], arr_in, *k_now], axis=0)
+    piece_now = jax.lax.axis_index(ax_name)
+    out_arr = len(block_out)
+    o_now = piece_now - out_arr
+    piece_next = piece_next[(jnp.arange(axis_len) - o_now) % axis_len]
+    return clear_modes(piece_next, which_dim)
+
+
+_play_fields = functools.partial(read_rates, ax_name="seq", which_dim=1)
 
 
 def sent_together(arrays, axis, dim, along):
@@ -93,7 +127,7 @@
     score_scale = 1.0 / math.sqrt(head_size)
     head_width = key_weight.shape[1]
     local_heads = head_width // head_size
-    normed = normalize_rows(lax.all_gather(caption_states, "seq", axis=1, tiled=True), caption_gain)
+    normed = normalize_rows(_play_fields(caption_states), caption_gain)
     normed_text = normed[0]
     caption_rows = normed_text.shape[0]
     pieces = sent_together((key_weight, value_weight), "dp", 0, 1)

time: 240 us -> 223 us (0.929)
  waiting for transfers between devices: 125 us -> 69.1 us
  starting transfers between devices: 7.62 us -> 29.8 us
  local copies, waits for them, and re-layouts: 16.8 us -> 33.2 us
  other arithmetic: 14.5 us -> 19.6 us
  blocking collectives: 34.7 us -> 30.7 us
    ppermute x0 -> x7, waiting for transfers between devices: none -> 53 us  [the longest x4 28.5 us: read_rates(): z = jax.lax.ppermute(block_out[-1] if block_out else arr_in, ax_name, inbox)]
    all_to_all x1, waiting for transfers between devices: 50.6 us -> 0.01 us  [side_by_side(): lax.all_to_all(both, axis, split_axis=split_dim, concat_axis=concat_dim,...]
    all_gather x1, waiting for transfers between devices: 45.8 us -> 0.01 us  [sent_together(): lax.all_gather(both, axis, axis=dim, tiled=True)]
    all_gather x1 -> x0, waiting for transfers between devices: 21 us -> none  [local(): lax.all_gather(caption_states, 'seq', axis=1, tiled=True)]
    ppermute x0 -> x7, starting transfers between devices: none -> 20.2 us  [the longest x4 11.7 us: read_rates(): z = jax.lax.ppermute(block_out[-1] if block_out else arr_in, ax_name, inbox)]
    unnamed x29 -> x44, local copies, waits for them, and re-layouts: 9.77 us -> 19.1 us
    reduce_scatter x1, waiting for transfers between devices: 6.91 us -> 16.1 us  [local(): lax.psum_scatter(lax.dot_general(columns, stacked, contract_rows, preferr...]
    convert_element_type x0 -> x1, other arithmetic: none -> 5.78 us  [normalize_rows(): (values * lax.rsqrt(mean_square + norm_epsilon) * caption_gain).astype(jn...]
  transfers between devices with their start and end apart: 4 -> 10, of which waited for: 4 -> 6; matrix products, arithmetic and copies ran while one was open for 15% -> 26% of each run, Pallas kernels for 0% -> 0%
where the time goes in v1:
time: 223 us; the launch traced here: 222 us
  waiting for transfers between devices  69.1 us (31%)
  local copies, waits for them, and re-layouts  33.2 us (15%)
  blocking collectives  30.7 us (14%)
  starting transfers between devices  29.8 us (13%)
  matrix products  25.1 us (11%)
  other arithmetic  19.6 us (9%)
  between operations  14.3 us (6%)
    all_to_all x1, blocking collectives, side_by_side(): lax.all_to_all(both, axis, split_axis=split_dim, concat_axis=concat_dim,...  30.7 us
    ppermute x4, waiting for transfers between devices, read_rates(): z = jax.lax.ppermute(block_out[-1] if block_out else arr_in, ax_name, inbox)  28.5 us
    ppermute x3, waiting for transfers between devices, read_rates(): jax.lax.ppermute(k_now[-1] if k_now else arr_in, perm=by_rank, axis_name=...  24.5 us
    unnamed x44, local copies, waits for them, and re-layouts  19.1 us
    reduce_scatter x1, waiting for transfers between devices, local(): lax.psum_scatter(lax.dot_general(columns, stacked, contract_rows, preferr...  16.1 us
    ppermute x4, starting transfers between devices, read_rates(): z = jax.lax.ppermute(block_out[-1] if block_out else arr_in, ax_name, inbox)  11.7 us
    all_to_all x1, starting transfers between devices, side_by_side(): lax.all_to_all(both, axis, split_axis=split_dim, concat_axis=concat_dim,...  9.51 us
    ppermute x3, starting transfers between devices, read_rates(): jax.lax.ppermute(k_now[-1] if k_now else arr_in, perm=by_rank, axis_name=...  8.48 us
  transfers between devices with their start and end apart: 10, of which 6 were waited for; matrix products, arithmetic and copies ran while one was open for 26% of the time, Pallas kernels for 0%

profile of v1, /device:TPU:12, one launch (start us, length us, event | category | flops | bytes accessed | tf_op | source)
XLA Modules:
  0.0 222.2 jit_solution(9378618968030740308)
XLA Ops:
  7.2 3.6 %collective-permute-start = (bf16[1,64,4096]{2,1,0:T(8,128)(2,1)}, bf16[1,64,4096]{2,1,0:T(8,128)(2,1)S(1)}, u32[]{:S(2)}, u32[]{:S(2)}) collective-permute-start(bf16[1,64,4096]{2,1,0:T(8,128)(2,1)} %param.22), channel_id=1, source_target_pairs={{0,16},{16,32},{32,48},{48,64},{64,80},{80,96},{96,112},{112,0},{1... | collective-permute-start | bytes 1572872 | tf_op jit(solution)/shard_map/ppermute | solution.py:28
  10.9 2.4 %collective-permute-start.4 = (bf16[1,64,4096]{2,1,0:T(8,128)(2,1)}, bf16[1,64,4096]{2,1,0:T(8,128)(2,1)S(1)}, u32[]{:S(2)}, u32[]{:S(2)}) collective-permute-start(bf16[1,64,4096]{2,1,0:T(8,128)(2,1)} %param.22), channel_id=1, source_target_pairs={{16,0},{32,16},{48,32},{64,48},{80,64},{96,80},{112,96},{0,112},{1... | collective-permute-start | bytes 1572872 | tf_op jit(solution)/shard_map/ppermute | solution.py:31
  13.2 9.9 %collective-permute-done = bf16[1,64,4096]{2,1,0:T(8,128)(2,1)S(1)} collective-permute-done((bf16[1,64,4096]{2,1,0:T(8,128)(2,1)}, bf16[1,64,4096]{2,1,0:T(8,128)(2,1)S(1)}, u32[]{:S(2)}, u32[]{:S(2)}) %collective-permute-start) | collective-permute-done | bytes 524320 | tf_op jit(solution)/shard_map/ppermute | solution.py:28
  23.1 3.5 %collective-permute-start.1 = (bf16[1,64,4096]{2,1,0:T(8,128)(2,1)S(1)}, bf16[1,64,4096]{2,1,0:T(8,128)(2,1)S(1)}, u32[]{:S(2)}, u32[]{:S(2)}) collective-permute-start(bf16[1,64,4096]{2,1,0:T(8,128)(2,1)S(1)} %collective-permute-done), channel_id=1, source_target_pairs={{0,16},{16,32},{32,48},{48,64},{64,80},{80,96},{96,112},{112,0},{1... | collective-permute-start | bytes 1572872 | tf_op jit(solution)/shard_map/ppermute | solution.py:28
  28.2 1.7 copy_dynamic-update-slice_fusion.5
  29.9 1.7 copy_dynamic-update-slice_fusion.4
  31.6 7.0 %collective-permute-done.1 = bf16[1,64,4096]{2,1,0:T(8,128)(2,1)S(1)} collective-permute-done((bf16[1,64,4096]{2,1,0:T(8,128)(2,1)S(1)}, bf16[1,64,4096]{2,1,0:T(8,128)(2,1)S(1)}, u32[]{:S(2)}, u32[]{:S(2)}) %collective-permute-start.1) | collective-permute-done | bytes 524320 | tf_op jit(solution)/shard_map/ppermute | solution.py:28
  38.6 2.7 %collective-permute-start.2 = (bf16[1,64,4096]{2,1,0:T(8,128)(2,1)S(1)}, bf16[1,64,4096]{2,1,0:T(8,128)(2,1)}, u32[]{:S(2)}, u32[]{:S(2)}) collective-permute-start(bf16[1,64,4096]{2,1,0:T(8,128)(2,1)S(1)} %collective-permute-done.1), channel_id=1, source_target_pairs={{0,16},{16,32},{32,48},{48,64},{64,80},{80,96},{96,112},{112,0},{1... | collective-permute-start | bytes 1572872 | tf_op jit(solution)/shard_map/ppermute | solution.py:28
  41.3 1.7 copy_dynamic-update-slice_fusion.3
  44.5 4.0 %collective-permute-start.5 = (bf16[1,64,4096]{2,1,0:T(8,128)(2,1)S(1)}, bf16[1,64,4096]{2,1,0:T(8,128)(2,1)}, u32[]{:S(2)}, u32[]{:S(2)}) collective-permute-start(bf16[1,64,4096]{2,1,0:T(8,128)(2,1)S(1)} %collective-permute-done.4), channel_id=1, source_target_pairs={{16,0},{32,16},{48,32},{64,48},{80,64},{96,80},{112,96},{0,112},{1... | collective-permute-start | bytes 1572872 | tf_op jit(solution)/shard_map/ppermute | solution.py:31
  48.5 5.5 %collective-permute-done.2 = bf16[1,64,4096]{2,1,0:T(8,128)(2,1)} collective-permute-done((bf16[1,64,4096]{2,1,0:T(8,128)(2,1)S(1)}, bf16[1,64,4096]{2,1,0:T(8,128)(2,1)}, u32[]{:S(2)}, u32[]{:S(2)}) %collective-permute-start.2) | collective-permute-done | bytes 524320 | tf_op jit(solution)/shard_map/ppermute | solution.py:28
  54.0 1.9 collective-permute-start.3
  56.7 9.5 %all-to-all-start = ((bf16[6,128,8,128]{3,1,0,2:T(8,128)(2,1)}), bf16[6,128,8,128]{3,1,0,2:T(8,128)(2,1)S(1)}, u32[]{:S(2)}, u32[]{:S(2)}) async-start(bf16[6,128,8,128]{3,1,0,2:T(8,128)(2,1)} %copy_dynamic-update-slice_fusion), calls=%async_computation | async-start | bytes 3145728 | tf_op jit(solution)/shard_map/all_to_all | solution.py:56
  68.3 2.1 collective-permute-start.6
  70.4 6.1 %collective-permute-done.3 = bf16[1,64,4096]{2,1,0:T(8,128)(2,1)} collective-permute-done((bf16[1,64,4096]{2,1,0:T(8,128)(2,1)}, bf16[1,64,4096]{2,1,0:T(8,128)(2,1)}, u32[]{:S(2)}, u32[]{:S(2)}) %collective-permute-start.3) | collective-permute-done | bytes 524320 | tf_op jit(solution)/shard_map/ppermute | solution.py:28
  76.5 1.9 bitcast_dynamic-update-slice_fusion.7
  78.4 1.9 bitcast_dynamic-update-slice_fusion.6
  83.7 1.9 bitcast_dynamic-update-slice_fusion.1
  85.6 24.5 %collective-permute-done.6 = bf16[1,64,4096]{2,1,0:T(8,128)(2,1)S(1)} collective-permute-done((bf16[1,64,4096]{2,1,0:T(8,128)(2,1)}, bf16[1,64,4096]{2,1,0:T(8,128)(2,1)S(1)}, u32[]{:S(2)}, u32[]{:S(2)}) %collective-permute-start.6) | collective-permute-done | bytes 524320 | tf_op jit(solution)/shard_map/ppermute | solution.py:31
  110.9 5.0 %gather_fusion = bf16[8,64,4096]{2,1,0:T(8,128)(2,1)} fusion(bf16[8,64,4096]{2,1,0:T(8,128)(2,1)} %bitcast.25, s32[1024]{0:T(1024)S(1)} %pad_clamp_fusion), kind=kCustom, calls=%fused_computation | custom fusion | bytes 8388640 | tf_op jit(solution)/shard_map/gather | solution.py:37
  115.9 3.1 %multiply_reduce_fusion.2 = f32[8,64]{1,0:T(8,128)S(1)} fusion(bf16[8,64,4096]{2,1,0:T(8,128)(2,1)} %gather_fusion), kind=kLoop, calls=%fused_computation.67 | loop fusion | flops 6290944 | bytes 4196352 | tf_op jit(solution)/shard_map/reduce_sum | solution.py:62
  119.1 5.8 %fusion.50 = bf16[512,4096]{1,0:T(8,128)(2,1)} fusion(f32[4096]{0:T(1024)S(1)} %copy-done.13, f32[512]{0:T(512)S(1)} %rsqrt.12, bf16[8,64,4096]{2,1,0:T(8,128)(2,1)} %gather_fusion), kind=kLoop, calls=%fused_computation.66 | loop fusion | flops 8388608 | bytes 8407040 | tf_op jit(solution)/shard_map/convert_element_type | solution.py:63
  126.8 3.9 %fusion.51 = bf16[512,1,128]{2,0,1:T(8,128)(2,1)S(1)} fusion(bf16[512,4096]{1,0:T(8,128)(2,1)} %fusion.50, bf16[4096,256]{1,0:T(8,128)(2,1)} %all-gather.2.cloned.1.call-done), kind=kOutput, calls=%fused_computation.72 | convolution fusion | flops 536936448 | bytes 5373952 | tf_op jit(solution)/shard_map/dot_general | solution.py:135
  130.7 3.2 %fusion.52 = bf16[512,1,128]{2,0,1:T(8,128)(2,1)} fusion(bf16[512,4096]{1,0:T(8,128)(2,1)S(1)} %copy-done, bf16[4096,256]{1,0:T(8,128)(2,1)} %all-gather.2.cloned.1.call-done), kind=kOutput, calls=%fused_computation.73 | convolution fusion | flops 536936448 | bytes 5373952 | tf_op jit(solution)/shard_map/dot_general | solution.py:136
  134.0 7.1 %while.31 = (s32[]{:T(128)}, f32[512,1,128]{0,2,1:T(8,128)S(1)}, f32[512,1,128]{0,2,1:T(8,128)S(1)}, bf16[2,512,1,128]{3,1,2,0:T(8,128)(2,1)S(1)}, bf16[2,512,1,...) while((s32[]{:T(128)}, f32[512,1,128]{0,2,1:T(8,128)S(1)}, ...), condition=%wide.region_10.11_spmd.clone, body=%wide.region_6.10_spmd.clone.sunk | while | flops 340524032 | bytes 11689132 | solution.py:108
  141.2 4.9 %convolution_convert_fusion = bf16[4096,256]{1,0:T(8,128)(2,1)} fusion(bf16[512,4096]{1,0:T(8,128)(2,1)} %fusion.50, bf16[512,128]{0,1:T(8,128)(2,1)S(1)} %get-tuple-element.309, bf16[512,128]{0,1:T(8,128)(2,1)S(1)} %get-tuple-element.310), kind=kOutput, calls=%fused_computation.68 | convolution fusion | flops 1075314688 | bytes 6553600 | tf_op jit(solution)/shard_map/dot_general | solution.py:180
  146.2 13.7 %while.30 = (s32[]{:T(128)}, f32[1024,1,128]{0,2,1:T(8,128)S(1)}, f32[1024,1,128]{0,2,1:T(8,128)}, bf16[2,512,1,128]{3,1,2,0:T(8,128)(2,1)S(1)}, bf16[2,512,1,12...) while((s32[]{:T(128)}, f32[1024,1,128]{0,2,1:T(8,128)S(1)}, ...), condition=%wide.region_4.5_spmd.clone, body=%wide.region_0.4_spmd.clone.sunk | while | flops 685243904 | bytes 23622340 | solution.py:108
  148.0 2.5 %fusion.102 = f32[1024,1,128]{0,2,1:T(8,128)} fusion(f32[1024,1,128]{0,2,1:T(8,128)} %get-tuple-element.483, pred[]{:T(512)S(6)} %compare.13, bf16[2,512,1,128]{3,1,2,0:T(8,128)(2,1)} %get-tuple-element.499, s32[]{:T(128)} %get-tuple-element.481, f32[512,1024]{1,0:T(8,128)S(1)} %get-tuple-element.420, f32[512]{0:T(512)S(1)} %fusion.100, ...), kind=kOutput, calls=%fused_computation.11.clone.1 | convolution fusion | flops 137101312 | bytes 3282433 | tf_op jit(solution)/shard_map/while/body/eval_jaxpr/hqk,qhd->khd/dot_general | solution.py:88
  154.8 2.7 %fusion.102 = f32[1024,1,128]{0,2,1:T(8,128)} fusion(f32[1024,1,128]{0,2,1:T(8,128)} %get-tuple-element.483, pred[]{:T(512)S(6)} %compare.13, bf16[2,512,1,128]{3,1,2,0:T(8,128)(2,1)} %get-tuple-element.499, s32[]{:T(128)} %get-tuple-element.481, f32[512,1024]{1,0:T(8,128)S(1)} %get-tuple-element.420, f32[512]{0:T(512)S(1)} %fusion.100, ...), kind=kOutput, calls=%fused_computation.11.clone.1 | convolution fusion | flops 137101312 | bytes 3282433 | tf_op jit(solution)/shard_map/while/body/eval_jaxpr/hqk,qhd->khd/dot_general | solution.py:88
  163.2 30.7 %all_to_all.30 = bf16[4,1024,1,128]{3,0,2,1:T(4,128)(2,1)S(1)} all-to-all(bf16[4,1024,1,128]{3,0,2,1:T(4,128)(2,1)S(1)} %copy.77), channel_id=1, replica_groups=mesh['section'=4,'seq'=8,'dp'=16] {'seq'}, dimensions={1} | all-to-all | bytes 2097152 | tf_op jit(solution)/shard_map/all_to_all | solution.py:56
  197.6 16.1 %reduce-scatter.2.cloned.1.call-done = bf16[256,256]{1,0:T(8,128)(2,1)} async-done(((bf16[4096,256]{1,0:T(8,128)(2,1)}), bf16[256,256]{1,0:T(8,128)(2,1)}) %reduce-scatter.2.cloned.1.call-update) | async-done | bytes 131088 | tf_op jit(solution)/shard_map/reduce_scatter | solution.py:179
  213.7 1.6 fusion.63
  (114 shorter events, 34.5 us)
Async XLA Ops:
  7.2 35.8 %copy-start.9 = (bf16[1,128,8,128]{3,2,1,0:T(8,128)(2,1)S(1)}, bf16[1,128,8,128]{3,2,1,0:T(8,128)(2,1)}, u32[]{:S(2)}) copy-start(bf16[1,128,8,128]{3,2,1,0:T(8,128)(2,1)} %param.19) | copy-start | bytes 786436
  7.2 36.6 %copy-start.10 = (bf16[1,128,8,128]{3,2,1,0:T(8,128)(2,1)S(1)}, bf16[1,128,8,128]{3,2,1,0:T(8,128)(2,1)}, u32[]{:S(2)}) copy-start(bf16[1,128,8,128]{3,2,1,0:T(8,128)(2,1)} %param.20) | copy-start | bytes 786436
  7.2 48.7 %copy-start.11 = (bf16[1,128,8,128]{3,2,1,0:T(8,128)(2,1)S(1)}, bf16[1,128,8,128]{3,2,1,0:T(8,128)(2,1)}, u32[]{:S(2)}) copy-start(bf16[1,128,8,128]{3,2,1,0:T(8,128)(2,1)} %param.21) | copy-start | bytes 786436
  7.2 119.6 %all-gather.2.cloned.1.call-start = ((), (), s32[]{:S(2)}) async-start(), calls=%async_computation.3 | async-start | bytes 2228224 | tf_op jit(solution)/shard_map/all_gather | solution.py:50
  7.2 15.9 %collective-permute-start = (bf16[1,64,4096]{2,1,0:T(8,128)(2,1)}, bf16[1,64,4096]{2,1,0:T(8,128)(2,1)S(1)}, u32[]{:S(2)}, u32[]{:S(2)}) collective-permute-start(bf16[1,64,4096]{2,1,0:T(8,128)(2,1)} %param.22), channel_id=1, source_target_pairs={{0,16},{16,32},{32,48},{48,64},{64,80},{80,96},{96,112},{112,0},{1... | collective-permute-start | bytes 1572872 | tf_op jit(solution)/shard_map/ppermute | solution.py:28
  10.9 33.7 %collective-permute-start.4 = (bf16[1,64,4096]{2,1,0:T(8,128)(2,1)}, bf16[1,64,4096]{2,1,0:T(8,128)(2,1)S(1)}, u32[]{:S(2)}, u32[]{:S(2)}) collective-permute-start(bf16[1,64,4096]{2,1,0:T(8,128)(2,1)} %param.22), channel_id=1, source_target_pairs={{16,0},{32,16},{48,32},{64,48},{80,64},{96,80},{112,96},{0,112},{1... | collective-permute-start | bytes 1572872 | tf_op jit(solution)/shard_map/ppermute | solution.py:31
  23.1 33.5 %copy-start.3 = (bf16[1,64,4096]{2,1,0:T(8,128)(2,1)}, bf16[1,64,4096]{2,1,0:T(8,128)(2,1)S(1)}, u32[]{:S(2)}) copy-start(bf16[1,64,4096]{2,1,0:T(8,128)(2,1)S(1)} %collective-permute-done) | copy-start | bytes 1572868
  23.1 15.4 %collective-permute-start.1 = (bf16[1,64,4096]{2,1,0:T(8,128)(2,1)S(1)}, bf16[1,64,4096]{2,1,0:T(8,128)(2,1)S(1)}, u32[]{:S(2)}, u32[]{:S(2)}) collective-permute-start(bf16[1,64,4096]{2,1,0:T(8,128)(2,1)S(1)} %collective-permute-done), channel_id=1, source_target_pairs={{0,16},{16,32},{32,48},{48,64},{64,80},{80,96},{96,112},{112,0},{1... | collective-permute-start | bytes 1572872 | tf_op jit(solution)/shard_map/ppermute | solution.py:28
  38.6 18.1 %copy-start.5 = (bf16[1,64,4096]{2,1,0:T(8,128)(2,1)}, bf16[1,64,4096]{2,1,0:T(8,128)(2,1)S(1)}, u32[]{:S(2)}) copy-start(bf16[1,64,4096]{2,1,0:T(8,128)(2,1)S(1)} %collective-permute-done.1) | copy-start | bytes 1572868
  38.6 15.4 %collective-permute-start.2 = (bf16[1,64,4096]{2,1,0:T(8,128)(2,1)S(1)}, bf16[1,64,4096]{2,1,0:T(8,128)(2,1)}, u32[]{:S(2)}, u32[]{:S(2)}) collective-permute-start(bf16[1,64,4096]{2,1,0:T(8,128)(2,1)S(1)} %collective-permute-done.1), channel_id=1, source_target_pairs={{0,16},{16,32},{32,48},{48,64},{64,80},{80,96},{96,112},{112,0},{1... | collective-permute-start | bytes 1572872 | tf_op jit(solution)/shard_map/ppermute | solution.py:28
  43.8 22.5 %copy-start.14 = (s32[16]{0:T(128)S(1)}, s32[16]{0:T(128)}, u32[]{:S(2)}) copy-start(s32[16]{0:T(128)} %param.26) | copy-start | bytes 196
  43.8 23.1 %copy-start.15 = (s32[16]{0:T(128)S(1)}, s32[16]{0:T(128)}, u32[]{:S(2)}) copy-start(s32[16]{0:T(128)} %param.27) | copy-start | bytes 196
  44.5 23.8 %collective-permute-start.5 = (bf16[1,64,4096]{2,1,0:T(8,128)(2,1)S(1)}, bf16[1,64,4096]{2,1,0:T(8,128)(2,1)}, u32[]{:S(2)}, u32[]{:S(2)}) collective-permute-start(bf16[1,64,4096]{2,1,0:T(8,128)(2,1)S(1)} %collective-permute-done.4), channel_id=1, source_target_pairs={{16,0},{32,16},{48,32},{64,48},{80,64},{96,80},{112,96},{0,112},{1... | collective-permute-start | bytes 1572872 | tf_op jit(solution)/shard_map/ppermute | solution.py:31
  54.0 22.5 %collective-permute-start.3 = (bf16[1,64,4096]{2,1,0:T(8,128)(2,1)}, bf16[1,64,4096]{2,1,0:T(8,128)(2,1)}, u32[]{:S(2)}, u32[]{:S(2)}) collective-permute-start(bf16[1,64,4096]{2,1,0:T(8,128)(2,1)} %collective-permute-done.2), channel_id=1, source_target_pairs={{0,16},{16,32},{32,48},{48,64},{64,80},{80,96},{96,112},{112,0},{1... | collective-permute-start | bytes 1572872 | tf_op jit(solution)/shard_map/ppermute | solution.py:28
  56.7 68.2 %all-to-all-start = ((bf16[6,128,8,128]{3,1,0,2:T(8,128)(2,1)}), bf16[6,128,8,128]{3,1,0,2:T(8,128)(2,1)S(1)}, u32[]{:S(2)}, u32[]{:S(2)}) async-start(bf16[6,128,8,128]{3,1,0,2:T(8,128)(2,1)} %copy_dynamic-update-slice_fusion), calls=%async_computation | async-start | bytes 3145728 | tf_op jit(solution)/shard_map/all_to_all | solution.py:56
  66.2 147.6 %reduce-scatter.2.cloned.1.call-start = ((), (), s32[]{:S(2)}) async-start(), calls=%async_computation.4 | async-start | bytes 2228224 | tf_op jit(solution)/shard_map/reduce_scatter | solution.py:179
  67.5 12.8 %copy-start.6 = (bf16[1,64,4096]{2,1,0:T(8,128)(2,1)S(1)}, bf16[1,64,4096]{2,1,0:T(8,128)(2,1)}, u32[]{:S(2)}) copy-start(bf16[1,64,4096]{2,1,0:T(8,128)(2,1)} %copy-done.5) | copy-start | bytes 1572868
  67.5 13.7 %copy-start.4 = (bf16[1,64,4096]{2,1,0:T(8,128)(2,1)S(1)}, bf16[1,64,4096]{2,1,0:T(8,128)(2,1)}, u32[]{:S(2)}) copy-start(bf16[1,64,4096]{2,1,0:T(8,128)(2,1)} %copy-done.3) | copy-start | bytes 1572868
  68.3 13.7 %copy-start.2 = (bf16[1,64,4096]{2,1,0:T(8,128)(2,1)S(1)}, bf16[1,64,4096]{2,1,0:T(8,128)(2,1)}, u32[]{:S(2)}) copy-start(bf16[1,64,4096]{2,1,0:T(8,128)(2,1)} %param.22) | copy-start | bytes 1572868
  68.3 41.8 %collective-permute-start.6 = (bf16[1,64,4096]{2,1,0:T(8,128)(2,1)}, bf16[1,64,4096]{2,1,0:T(8,128)(2,1)S(1)}, u32[]{:S(2)}, u32[]{:S(2)}) collective-permute-start(bf16[1,64,4096]{2,1,0:T(8,128)(2,1)} %collective-permute-done.5), channel_id=1, source_target_pairs={{16,0},{32,16},{48,32},{64,48},{80,64},{96,80},{112,96},{0,112},{1... | collective-permute-start | bytes 1572872 | tf_op jit(solution)/shard_map/ppermute | solution.py:31
  115.9 3.2 %copy-start.13 = (f32[4096]{0:T(1024)S(1)}, f32[4096]{0:T(1024)}, u32[]{:S(2)}) copy-start(f32[4096]{0:T(1024)} %param.23) | copy-start | bytes 49156
  126.8 3.9 %copy-start = (bf16[512,4096]{1,0:T(8,128)(2,1)S(1)}, bf16[512,4096]{1,0:T(8,128)(2,1)}, u32[]{:S(2)}) copy-start(bf16[512,4096]{1,0:T(8,128)(2,1)} %fusion.50) | copy-start | bytes 12582916
  130.7 3.2 %copy-start.8 = (f32[512,1,128]{0,2,1:T(8,128)S(1)}, f32[512,1,128]{0,2,1:T(8,128)}, u32[]{:S(2)}) copy-start(f32[512,1,128]{0,2,1:T(8,128)} %custom-call.3) | copy-start | bytes 786436
  135.3 0.9 copy-start.16
  138.8 0.9 copy-start.16
  141.1 5.0 %copy-start.1 = (bf16[2,512,1,128]{3,1,2,0:T(8,128)(2,1)}, bf16[2,512,1,128]{3,1,2,0:T(8,128)(2,1)S(1)}, u32[]{:S(2)}) copy-start(bf16[2,512,1,128]{3,1,2,0:T(8,128)(2,1)S(1)} %get-tuple-element.107) | copy-start | bytes 786436
  148.0 2.5 %copy-start.7 = (bf16[1024,1,128]{2,0,1:T(8,128)(2,1)S(1)}, bf16[1024,1,128]{2,0,1:T(8,128)(2,1)}, u32[]{:S(2)}) copy-start(bf16[1024,1,128]{2,0,1:T(8,128)(2,1)} %get-tuple-element.500) | copy-start | bytes 786436 | tf_op jit(solution)/shard_map/while
  148.0 2.5 %copy-start.12 = (bf16[2,512,1,128]{3,1,2,0:T(8,128)(2,1)S(1)}, bf16[2,512,1,128]{3,1,2,0:T(8,128)(2,1)}, u32[]{:S(2)}) copy-start(bf16[2,512,1,128]{3,1,2,0:T(8,128)(2,1)} %get-tuple-element.499) | copy-start | bytes 786436 | tf_op jit(solution)/shard_map/while
  154.7 2.7 %copy-start.7 = (bf16[1024,1,128]{2,0,1:T(8,128)(2,1)S(1)}, bf16[1024,1,128]{2,0,1:T(8,128)(2,1)}, u32[]{:S(2)}) copy-start(bf16[1024,1,128]{2,0,1:T(8,128)(2,1)} %get-tuple-element.500) | copy-start | bytes 786436 | tf_op jit(solution)/shard_map/while
  154.7 2.7 %copy-start.12 = (bf16[2,512,1,128]{3,1,2,0:T(8,128)(2,1)S(1)}, bf16[2,512,1,128]{3,1,2,0:T(8,128)(2,1)}, u32[]{:S(2)}) copy-start(bf16[2,512,1,128]{3,1,2,0:T(8,128)(2,1)} %get-tuple-element.499) | copy-start | bytes 786436 | tf_op jit(solution)/shard_map/while
Sparse Core Ops, SparseCore 0:
  28.3 47.4 all-gather.1
  146.2 67.4 reduce-scatter.1
